TPU v7x, 128 devices: a whole 4x4x4 slice. The times are simulated.
128 devices in a mesh: gx: 16 (over x, y), gy: 4 (over z), gz: 2 (over core).
Axes of the slice: x: 4, y: 4, z: 4, core: 2. Of those that a mesh axis runs over, the one named last changes fastest.
Arguments:
- conserved: float32 [14, 128, 256, 512], P(None, 'gx', 'gy', 'gz')
- char_left: float32 [14, 14], replicated
- char_right: float32 [14, 14], replicated
- shock_list: int32 [16, 4, 2, 128], P('gx', 'gy', 'gz'), may hold values from 0 to 511, as said below
- shock_count: int32 [16, 4, 2], P('gx', 'gy', 'gz'), may hold values from 32 to 128, as said below
Outputs:
- advanced: float32 [14, 128, 256, 512], P(None, 'gx', 'gy', 'gz')
Inputs may be any that keep to these rules, and one draw needn't show every extreme that they name: `shock_list`: the entries of one device's list are distinct local pencil indices; only the first shock_count of them are shocked pencils. `shock_count`: in every column of devices along gx (fixed gy and gz index) one device has 128 shocked pencils and every other device has 32, so a column holds 608 in all.
All inputs are finite; a program needn't handle non-finite values.
Results may differ from a plain program's by a relative error of at most 0.00005.
Values sent between devices are 32-bit elements; how exact they have to be, the bound alone decides.
A program may use at most 192 MiB of HBM per device.

v0:
```python
import jax
import jax.numpy as jnp
from jax import lax
from jax.sharding import PartitionSpec as P

SPECIES = 9
VARIABLES = 14


gas_excess = 0.4
time_step = 0.2
weno_epsilon = 1e-06


def extended(cells, sides, width):
    for axis, dim in sides:
        count = lax.axis_size(axis)
        head = lax.slice_in_dim(cells, 0, width, axis=dim)
        tail = lax.slice_in_dim(cells, cells.shape[dim] - width, cells.shape[dim], axis=dim)
        cells = jnp.concatenate(
            [
                lax.ppermute(tail, axis, [(i, (i + 1) % count) for i in range(count)]),
                cells,
                lax.ppermute(head, axis, [((i + 1) % count, i) for i in range(count)]),
            ],
            axis=dim,
        )
    return cells


def directed_flux(values_in, normal):
    density = jnp.sum(values_in[:SPECIES], axis=0)
    inverse = 1.0 / density
    velocity = values_in[SPECIES + normal] * inverse
    momenta = values_in[SPECIES : SPECIES + 3]
    kinetic = 0.5 * jnp.sum(momenta * momenta, axis=0) * inverse
    pressure = gas_excess * (values_in[SPECIES + 3] - values_in[SPECIES + 4] - kinetic)
    component = jnp.arange(VARIABLES, dtype=jnp.int32)
    extra_shape = (VARIABLES,) + (1,) * (values_in.ndim - 1)
    normal_pick = (component == SPECIES + normal).astype(jnp.float32).reshape(extra_shape)
    energy_pick = (component == SPECIES + 3).astype(jnp.float32).reshape(extra_shape)
    result = values_in * velocity[None] + normal_pick * pressure[None]
    return result + energy_pick * (pressure * velocity)[None]


def central_difference(values_in, dimension, length_cells):

    def shifted(begin_at):
        return lax.slice_in_dim(values_in, begin_at, begin_at + length_cells, axis=dimension)

    return (
        45.0 * (shifted(4) - shifted(2))
        - 9.0 * (shifted(5) - shifted(1))
        + (shifted(6) - shifted(0))
    ) / 60.0


def upwind_value(first_cell, second_cell, middle, fourth_cell, fifth_cell):
    stencil_zero = (2.0 * first_cell - 7.0 * second_cell + 11.0 * middle) / 6.0
    stencil_one = (-second_cell + 5.0 * middle + 2.0 * fourth_cell) / 6.0
    stencil_two = (2.0 * middle + 5.0 * fourth_cell - fifth_cell) / 6.0
    smooth_zero = (
        13.0 / 12.0 * (first_cell - 2.0 * second_cell + middle) ** 2
        + 0.25 * (first_cell - 4.0 * second_cell + 3.0 * middle) ** 2
    )
    smooth_one = (
        13.0 / 12.0 * (second_cell - 2.0 * middle + fourth_cell) ** 2
        + 0.25 * (second_cell - fourth_cell) ** 2
    )
    smooth_two = (
        13.0 / 12.0 * (middle - 2.0 * fourth_cell + fifth_cell) ** 2
        + 0.25 * (3.0 * middle - 4.0 * fourth_cell + fifth_cell) ** 2
    )
    weight_zero = 0.1 / (weno_epsilon + smooth_zero) ** 2
    weight_one = 0.6 / (weno_epsilon + smooth_one) ** 2
    weight_two = 0.3 / (weno_epsilon + smooth_two) ** 2
    return (weight_zero * stencil_zero + weight_one * stencil_one + weight_two * stencil_two) / (
        weight_zero + weight_one + weight_two
    )


def weno_divergence(pencils, char_left, char_right):
    fluxes = directed_flux(pencils, 2)
    density = jnp.sum(pencils[:SPECIES], axis=0)
    wave_speed = jnp.max(jnp.abs(pencils[SPECIES + 2] / density), axis=-1) + 1.0
    outward = 0.5 * (fluxes + wave_speed[None, :, None] * pencils)
    inward = 0.5 * (fluxes - wave_speed[None, :, None] * pencils)
    char_out = jnp.einsum("ij,jpk->ipk", char_left, outward, precision=lax.Precision.HIGHEST)
    char_in = jnp.einsum("ij,jpk->ipk", char_left, inward, precision=lax.Precision.HIGHEST)
    face_count = pencils.shape[-1] - 5

    def window(values_in, begin_at):
        return values_in[..., begin_at : begin_at + face_count]

    summed = upwind_value(
        window(char_out, 0),
        window(char_out, 1),
        window(char_out, 2),
        window(char_out, 3),
        window(char_out, 4),
    )
    summed = summed + upwind_value(
        window(char_in, 5),
        window(char_in, 4),
        window(char_in, 3),
        window(char_in, 2),
        window(char_in, 1),
    )
    face_values = jnp.einsum("ij,jpk->ipk", char_right, summed, precision=lax.Precision.HIGHEST)
    return face_values[..., 1:] - face_values[..., :-1]


def on_device(conserved, char_left, char_right, shock_list, shock_count):
    cells_x = conserved.shape[1]
    cells_y = conserved.shape[2]
    cells_z = conserved.shape[3]
    pencil_total = cells_x * cells_y
    shock_max = shock_list.shape[-1]
    widened = extended(conserved, (("gy", 2), ("gz", 3)), 3)
    along_y = widened[:, :, :, 3 : 3 + cells_z]
    along_z = widened[:, :, 3 : 3 + cells_y, :]
    y_term = central_difference(directed_flux(along_y, 1), 2, cells_y)
    z_term = central_difference(directed_flux(along_z, 2), 3, cells_z)
    wide_rows = widened.reshape(VARIABLES, cells_x * (cells_y + 6), cells_z + 6)

    def framed_pencils(indices):
        rows = indices // cells_y * (cells_y + 6) + indices % cells_y + 3
        return jnp.take(wide_rows, rows, axis=1)

    shocked = shock_list.reshape(shock_max)
    live_count = shock_count.reshape(())
    slot_index = jnp.arange(shock_max, dtype=jnp.int32)
    helpers = lax.axis_size("gx")
    column_total = shock_max * (helpers + 3) // 4
    capacity = (column_total + helpers - 1) // helpers
    spill = max(1, (shock_max - capacity + helpers - 1) // helpers)
    kept_slots = framed_pencils(shocked[:capacity])
    spill_index = jnp.arange(helpers * spill, dtype=jnp.int32) + capacity
    spill_live = spill_index < live_count
    spill_source = jnp.take(shocked, jnp.clip(spill_index, 0, shock_max - 1))
    outgoing = jnp.where(spill_live[None, :, None], framed_pencils(spill_source), 0.0)
    incoming = lax.all_to_all(outgoing, "gx", split_axis=1, concat_axis=1, tiled=True)
    arrived = incoming.reshape(VARIABLES, helpers, spill, cells_z + 6).sum(axis=1)
    arrived_density = jnp.sum(arrived[:SPECIES], axis=0)
    arrived = jnp.where((arrived_density > 0.0)[None], arrived, 1.0)
    together = jnp.concatenate([kept_slots, arrived], axis=1)
    results = weno_divergence(together, char_left, char_right)
    kept_terms = results[:, :capacity]
    spill_terms = results[:, capacity:]
    answered = lax.all_to_all(
        jnp.tile(spill_terms, (1, helpers, 1)), "gx", split_axis=1, concat_axis=1, tiled=True
    )
    replaced = jnp.concatenate([kept_terms, answered], axis=1)[:, :shock_max]
    target = jnp.where(slot_index < live_count, shocked, pencil_total)
    pencil_ids = jnp.arange(pencil_total, dtype=jnp.int32)
    matches = (target[None, :] == pencil_ids[:, None]).astype(jnp.int32)
    hit_any = jnp.sum(matches, axis=1) > 0
    slot_of = jnp.sum(matches * slot_index[None, :], axis=1)
    picked = jnp.take(replaced, slot_of, axis=1).reshape(z_term.shape)
    hit_cells = hit_any.reshape(1, cells_x, cells_y, 1)
    z_final = jnp.where(hit_cells, picked, z_term)
    return conserved - time_step * (y_term + z_final)


def solution(mesh):
    placed = (P(None, "gx", "gy", "gz"), P(), P(), P("gx", "gy", "gz", None), P("gx", "gy", "gz"))
    return jax.shard_map(
        on_device, mesh=mesh, in_specs=placed, out_specs=P(None, "gx", "gy", "gz"), check_vma=False
    )
```

profile of v0, /device:TPU:3, one launch (start us, length us, event | category | flops | bytes accessed | tf_op | source)
XLA Modules:
  0.0 313.7 jit_solution(766375619921250858)
XLA Ops:
  0.0 1.7 fusion.241
  1.8 3.8 %collective-permute-start.1 = (f32[14,8,3,256]{3,1,2,0:T(8,128)S(1)}, f32[14,8,3,256]{3,1,2,0:T(8,128)S(1)}, u32[]{:S(2)}, u32[]{:S(2)}) collective-permute-start(f32[14,8,3,256]{3,1,2,0:T(8,128)S(1)} %copy.49), channel_id=1, source_target_pairs={{2,0},{4,2},{6,4},{0,6},{3,1},{5,3},{7,5},{1,7},{10,8},{12,10},{14... | collective-permute-start | bytes 1032200 | tf_op jit(solution)/shard_map/ppermute | solution.py:24
  8.1 11.2 %copy.39 = f32[14,8,64,256]{2,1,3,0:T(8,128)} copy(f32[14,8,64,256]{3,2,1,0:T(8,128)} %param.5) | data formatting | bytes 14680064 | tf_op args[0]
  19.4 7.6 %copy.30 = f32[14,8,3,256]{2,1,3,0:T(8,128)} copy(f32[14,8,3,256]{3,1,2,0:T(8,128)S(1)} %collective-permute-done) | data formatting | bytes 688128 | tf_op jit(solution)/shard_map/ppermute | solution.py:22
  27.1 7.6 %copy.32 = f32[14,8,3,256]{2,1,3,0:T(8,128)} copy(f32[14,8,3,256]{3,1,2,0:T(8,128)S(1)} %collective-permute-done.1) | data formatting | bytes 688128 | tf_op jit(solution)/shard_map/ppermute | solution.py:24
  34.7 21.2 %pad_maximum_fusion.1 = f32[14,8,70,256]{2,1,3,0:T(8,128)} fusion(f32[14,8,3,256]{2,1,3,0:T(8,128)} %copy.32, f32[14,8,64,256]{2,1,3,0:T(8,128)} %copy.39, f32[14,8,3,256]{2,1,3,0:T(8,128)} %copy.30), kind=kLoop, calls=%fused_computation.28 | loop fusion | flops 4014080 | bytes 16056320 | tf_op jit(solution)/shard_map/concatenate | solution.py:20
  55.9 1.4 fusion.240
  57.3 2.5 fusion.17
  59.8 4.5 %slice_reduce_fusion.1 = f32[8,70,256]{1,0,2:T(8,128)S(1)} fusion(f32[14,8,70,256]{2,1,3,0:T(8,128)} %pad_maximum_fusion.1), kind=kLoop, calls=%fused_computation.31 | loop fusion | flops 1146880 | bytes 5734400 | tf_op jit(solution)/shard_map/reduce_sum | solution.py:32
  65.5 2.2 multiply_bitcast_fusion.1
  67.8 16.9 %multiply_add_fusion = f32[14,8,70,256]{2,1,3,0:T(8,128)} fusion(f32[8,70,256]{1,0,2:T(8,128)S(1)} %get-tuple-element.11, f32[14]{0:T(128)S(1)} %get-tuple-element.22, f32[8,70,256]{1,0,2:T(8,128)S(1)} %bitcast.132, f32[14]{0:T(128)S(1)} %compare_convert_fusion.2, f32[8,70,256]{1,0,2:T(8,128)S(1)} %get-tuple-element.16, f32[14,8,3,256]{2,1,3,0:T(8,128)} %copy.32, ...), kind=kLoop, calls=%fused_computation.29 | loop fusion | flops 14049280 | bytes 17776752 | tf_op jit(solution)/shard_map/add | solution.py:43
  84.7 17.1 %pad_maximum_fusion = f32[14,8,70,262]{2,1,3,0:T(8,128)} fusion(f32[14,8,70,3]{2,1,3,0:T(8,128)S(1)} %collective-permute-done.3, f32[14,8,3,256]{2,1,3,0:T(8,128)} %copy.32, f32[14,8,64,256]{2,1,3,0:T(8,128)S(1)} %bitcast.126, f32[14,8,3,256]{2,1,3,0:T(8,128)} %copy.30, f32[14,8,70,3]{2,1,3,0:T(8,128)S(1)} %collective-permute-done.2), kind=kLoop, calls=%fused_computation.7 | loop fusion | flops 8216320 | bytes 16432640 | tf_op jit(solution)/shard_map/concatenate | solution.py:20
  101.8 13.7 %copy.44 = f32[14,8,70,262]{3,0,2,1:T(8,128)} copy(f32[14,8,70,262]{2,1,3,0:T(8,128)} %pad_maximum_fusion) | data formatting | bytes 16432640 | tf_op jit(solution)/shard_map/reshape | solution.py:124
  115.5 6.5 %gather_fusion = f32[38,14,262]{2,1,0:T(8,128)} fusion(f32[14,560,262]{2,0,1:T(8,128)} %bitcast.128, s32[1024]{0:T(1024)S(1)} %pad_clamp_fusion.3), kind=kCustom, calls=%fused_computation | custom fusion | bytes 1115224 | tf_op jit(solution)/shard_map/jit(_take)/gather | solution.py:128
  122.0 5.6 %gather_fusion.2 = f32[96,14,262]{2,1,0:T(8,128)S(1)} fusion(f32[14,560,262]{2,0,1:T(8,128)} %bitcast.129, s32[1024]{0:T(1024)S(1)} %pad_clamp_fusion.1), kind=kCustom, calls=%fused_computation.2 | custom fusion | bytes 2817408 | tf_op jit(solution)/shard_map/jit(_take)/gather | solution.py:128
  127.6 1.7 select_bitcast_fusion
  129.3 6.9 %all-to-all-start = ((f32[14,96,262]{2,0,1:T(8,128)}), f32[14,96,262]{2,0,1:T(8,128)S(1)}, u32[]{:S(2)}, u32[]{:S(2)}) async-start(f32[14,96,262]{2,0,1:T(8,128)} %select_bitcast_fusion), calls=%async_computation | async-start | bytes 4718592 | tf_op jit(solution)/shard_map/all_to_all | solution.py:142
  136.3 2.9 fusion.16
  139.4 6.4 %slice_reduce_fusion = f32[8,64,262]{1,0,2:T(8,128)S(1)} fusion(f32[14,8,70,262]{2,1,3,0:T(8,128)} %pad_maximum_fusion), kind=kLoop, calls=%fused_computation.30 | loop fusion | flops 1073152 | bytes 5365760 | tf_op jit(solution)/shard_map/reduce_sum | solution.py:32
  145.7 4.5 %multiply_bitcast_fusion = (f32[8,64,262]{1,0,2:T(8,128)}, f32[1,8,64,262]{2,1,3,0:T(8,128)}, f32[8,64,262]{1,0,2:T(8,128)}) fusion(f32[8,64,262]{1,0,2:T(8,128)S(1)} %slice_reduce_fusion, f32[14,8,70,262]{2,1,3,0:T(8,128)} %pad_maximum_fusion, f32[8,64,262]{1,0,2:T(8,128)S(1)} %fusion.16), kind=kLoop, calls=%fused_computation.203 | loop fusion | flops 1073152 | bytes 4292608 | tf_op jit(solution)/shard_map/mul | solution.py:43
  150.3 16.2 %all-to-all-done = f32[14,96,262]{2,0,1:T(8,128)S(1)} async-done(((f32[14,96,262]{2,0,1:T(8,128)}), f32[14,96,262]{2,0,1:T(8,128)S(1)}, u32[]{:S(2)}, u32[]{:S(2)}) %all-to-all-start) | async-done | bytes 1408544 | tf_op jit(solution)/shard_map/all_to_all | solution.py:142
  167.7 1.4 convolution_bitcast_fusion.1
  169.1 1.4 convolution_bitcast_fusion.2
  170.6 7.1 %convolution_bitcast_fusion = f32[14,44,257]{2,0,1:T(8,128)S(1)} fusion(f32[14,44,262]{2,0,1:T(8,128)S(1)} %convolution_bitcast_fusion.1, f32[14,44,262]{2,0,1:T(8,128)S(1)} %convolution_bitcast_fusion.2, f32[14,14]{1,0:T(8,128)S(1)} %copy-done.8), kind=kOutput, calls=%fused_computation.44 | convolution fusion | flops 47018664 | bytes 11454880 | tf_op jit(solution)/shard_map/ij,jpk->ipk/dot_general | solution.py:109
  179.3 7.7 %all-to-all-start.1 = ((f32[14,96,256]{2,0,1:T(8,128)}), f32[14,96,256]{2,0,1:T(8,128)}, u32[]{:S(2)}, u32[]{:S(2)}) async-start(f32[14,96,256]{2,0,1:T(8,128)} %bitcast.22), calls=%async_computation.1 | async-start | bytes 3145728 | tf_op jit(solution)/shard_map/all_to_all | solution.py:150
  187.0 11.9 %fusion.1 = f32[14,8,64,262]{2,1,3,0:T(8,128)} fusion(f32[14,8,70,262]{2,1,3,0:T(8,128)} %pad_maximum_fusion, f32[8,64,262]{1,0,2:T(8,128)S(1)} %copy-done.3, f32[14]{0:T(128)S(1)} %get-tuple-element.22, f32[8,64,262]{1,0,2:T(8,128)S(1)} %bitcast.131, f32[14]{0:T(128)S(1)} %get-tuple-element.21, f32[8,64,262]{1,0,2:T(8,128)S(1)} %copy-done.5), kind=kLoop, calls=%fused_computation.6 | loop fusion | flops 9390080 | bytes 16633968 | tf_op jit(solution)/shard_map/add | solution.py:43
  199.0 7.0 %all-to-all-done.1 = f32[14,96,256]{2,0,1:T(8,128)} async-done(((f32[14,96,256]{2,0,1:T(8,128)}), f32[14,96,256]{2,0,1:T(8,128)}, u32[]{:S(2)}, u32[]{:S(2)}) %all-to-all-start.1) | async-done | bytes 1376288 | tf_op jit(solution)/shard_map/all_to_all | solution.py:150
  206.0 1.6 pad_maximum_fusion.3
  207.6 4.4 %gather_fusion.3 = f32[512,14,256]{2,1,0:T(8,128)} fusion(f32[14,128,256]{2,0,1:T(8,128)S(1)} %pad_maximum_fusion.3, s32[1024]{0:T(1024)S(1)} %pad_clamp_fusion), kind=kCustom, calls=%fused_computation.3 | custom fusion | bytes 14682112 | tf_op jit(solution)/shard_map/jit(_take)/gather | solution.py:159
  212.0 10.8 %copy.38 = f32[14,8,64,256]{2,1,3,0:T(8,128)} copy(f32[14,8,64,256]{3,0,2,1:T(8,128)} %bitcast.127) | data formatting | bytes 14680064 | tf_op jit(solution)/shard_map/jit(_take)/gather | solution.py:159
  222.8 78.8 %fusion.7 = f32[14,8,64,256]{2,1,3,0:T(8,128)} fusion(f32[14,8,64,256]{2,1,3,0:T(8,128)} %copy.39, f32[14,8,64,262]{2,1,3,0:T(8,128)} %fusion.1, f32[14,8,70,256]{2,1,3,0:T(8,128)} %multiply_add_fusion, f32[14,8,64,256]{2,1,3,0:T(8,128)} %copy.38, pred[8,64]{1,0:T(8,128)(4,1)S(1)} %compare_and_fusion, pred[8,64]{1,0:T(8,128)(4,1)S(1)} %gt.29), kind=kLoop, calls=%fused_computation.14 | loop fusion | flops 38535168 | bytes 110101504 | tf_op jit(solution)/shard_map/sub | solution.py:162
  301.7 12.0 %copy.40 = f32[14,8,64,256]{3,2,1,0:T(8,128)} copy(f32[14,8,64,256]{2,1,3,0:T(8,128)} %fusion.7) | data formatting | bytes 14680064 | tf_op jit(solution)/shard_map/sub | solution.py:162
  (75 shorter events, 6.2 us)
Async XLA Ops:
  0.0 167.7 %copy-start = (f32[14,14]{1,0:T(8,128)S(1)}, f32[14,14]{1,0:T(8,128)}, u32[]{:S(2)}) copy-start(f32[14,14]{1,0:T(8,128)} %param.6) | copy-start | bytes 2356
  1.7 4.1 %copy-start.2 = (s32[1,1,1,128]{3,2,1,0:T(1,128)S(1)}, s32[1,1,1,128]{3,2,1,0:T(1,128)}, u32[]{:S(2)}) copy-start(s32[1,1,1,128]{3,2,1,0:T(1,128)} %param.8) | copy-start | bytes 1540
  1.8 25.3 %collective-permute-start.1 = (f32[14,8,3,256]{3,1,2,0:T(8,128)S(1)}, f32[14,8,3,256]{3,1,2,0:T(8,128)S(1)}, u32[]{:S(2)}, u32[]{:S(2)}) collective-permute-start(f32[14,8,3,256]{3,1,2,0:T(8,128)S(1)} %copy.49), channel_id=1, source_target_pairs={{2,0},{4,2},{6,4},{0,6},{3,1},{5,3},{7,5},{1,7},{10,8},{12,10},{14... | collective-permute-start | bytes 1032200 | tf_op jit(solution)/shard_map/ppermute | solution.py:24
  5.6 13.8 %collective-permute-start = (f32[14,8,3,256]{3,1,2,0:T(8,128)S(1)}, f32[14,8,3,256]{3,1,2,0:T(8,128)S(1)}, u32[]{:S(2)}, u32[]{:S(2)}) collective-permute-start(f32[14,8,3,256]{3,1,2,0:T(8,128)S(1)} %copy.48), channel_id=1, source_target_pairs={{0,2},{2,4},{4,6},{6,0},{1,3},{3,5},{5,7},{7,1},{8,10},{10,12},{12... | collective-permute-start | bytes 1032200 | tf_op jit(solution)/shard_map/ppermute | solution.py:22
  34.7 33.1 %slice-start = ((s8[14680064]{0:T(1024)(128)(4,1)}), s8[4194304]{0:T(1024)(128)(4,1)S(1)}, s32[]{:S(2)}) async-start(s8[14680064]{0:T(1024)(128)(4,1)} %bitcast.125), calls=%async_computation.2 | async-start | bytes 8388608
  34.7 33.1 %slice-start.1 = ((s8[14680064]{0:T(1024)(128)(4,1)}), s8[4194304]{0:T(1024)(128)(4,1)S(1)}, s32[]{:S(2)}) async-start(s8[14680064]{0:T(1024)(128)(4,1)} %bitcast.125), calls=%async_computation.3 | async-start | bytes 8388608
  34.7 33.1 %slice-start.2 = ((s8[14680064]{0:T(1024)(128)(4,1)}), s8[4194304]{0:T(1024)(128)(4,1)S(1)}, s32[]{:S(2)}) async-start(s8[14680064]{0:T(1024)(128)(4,1)} %bitcast.125), calls=%async_computation.4 | async-start | bytes 8388608
  57.3 10.5 %slice-start.3 = ((s8[14680064]{0:T(1024)(128)(4,1)}), s8[2097152]{0:T(1024)(128)(4,1)S(1)}, s32[]{:S(2)}) async-start(s8[14680064]{0:T(1024)(128)(4,1)} %bitcast.125), calls=%async_computation.5 | async-start | bytes 4194304
  64.2 20.5 %collective-permute-start.2 = (f32[14,8,70,3]{2,1,3,0:T(8,128)S(1)}, f32[14,8,70,3]{2,1,3,0:T(8,128)S(1)}, u32[]{:S(2)}, u32[]{:S(2)}) collective-permute-start(f32[14,8,70,3]{2,1,3,0:T(8,128)S(1)} %get-tuple-element.17), channel_id=1, source_target_pairs={{0,1},{1,0},{2,3},{3,2},{4,5},{5,4},{6,7},{7,6},{8,9},{9,8},{10,11... | collective-permute-start | bytes 282248 | tf_op jit(solution)/shard_map/ppermute | solution.py:22
  65.3 19.4 %collective-permute-start.3 = (f32[14,8,70,3]{2,1,3,0:T(8,128)S(1)}, f32[14,8,70,3]{2,1,3,0:T(8,128)S(1)}, u32[]{:S(2)}, u32[]{:S(2)}) collective-permute-start(f32[14,8,70,3]{2,1,3,0:T(8,128)S(1)} %get-tuple-element.18), channel_id=1, source_target_pairs={{1,0},{0,1},{3,2},{2,3},{5,4},{4,5},{7,6},{6,7},{9,8},{8,9},{11,10... | collective-permute-start | bytes 282248 | tf_op jit(solution)/shard_map/ppermute | solution.py:24
  129.3 37.1 %all-to-all-start = ((f32[14,96,262]{2,0,1:T(8,128)}), f32[14,96,262]{2,0,1:T(8,128)S(1)}, u32[]{:S(2)}, u32[]{:S(2)}) async-start(f32[14,96,262]{2,0,1:T(8,128)} %select_bitcast_fusion), calls=%async_computation | async-start | bytes 4718592 | tf_op jit(solution)/shard_map/all_to_all | solution.py:142
  136.3 3.0 copy-start.6
  169.1 1.4 copy-start.8
  177.9 1.4 copy-start.7
  177.9 9.1 %copy-start.5 = (f32[8,64,262]{1,0,2:T(8,128)S(1)}, f32[8,64,262]{1,0,2:T(8,128)}, u32[]{:S(2)}) copy-start(f32[8,64,262]{1,0,2:T(8,128)} %get-tuple-element.15) | copy-start | bytes 1609732
  179.3 7.7 %copy-start.3 = (f32[8,64,262]{1,0,2:T(8,128)S(1)}, f32[8,64,262]{1,0,2:T(8,128)}, u32[]{:S(2)}) copy-start(f32[8,64,262]{1,0,2:T(8,128)} %get-tuple-element.13) | copy-start | bytes 1609732
  179.3 7.7 %copy-start.4 = (f32[1,8,64,262]{2,1,3,0:T(8,128)S(1)}, f32[1,8,64,262]{2,1,3,0:T(8,128)}, u32[]{:S(2)}) copy-start(f32[1,8,64,262]{2,1,3,0:T(8,128)} %get-tuple-element.14) | copy-start | bytes 1609732
  179.3 26.7 %all-to-all-start.1 = ((f32[14,96,256]{2,0,1:T(8,128)}), f32[14,96,256]{2,0,1:T(8,128)}, u32[]{:S(2)}, u32[]{:S(2)}) async-start(f32[14,96,256]{2,0,1:T(8,128)} %bitcast.22), calls=%async_computation.1 | async-start | bytes 3145728 | tf_op jit(solution)/shard_map/all_to_all | solution.py:150
  199.0 7.0 %slice-start.4 = ((f32[14,44,256]{2,0,1:T(8,128)}), f32[14,38,256]{2,0,1:T(8,128)S(1)}, s32[]{:S(2)}) async-start(f32[14,44,256]{2,0,1:T(8,128)} %copy-done.7), calls=%async_computation.6 | async-start | bytes 1245184 | tf_op jit(solution)/shard_map/slice | solution.py:148
  301.7 12.0 %copy-start.1 = (f32[14,14]{1,0:T(8,128)S(1)}, f32[14,14]{1,0:T(8,128)}, u32[]{:S(2)}) copy-start(f32[14,14]{1,0:T(8,128)} %param.6) | copy-start | bytes 2356
where the time goes:
time: 320 us; the launch traced here: 314 us
  other arithmetic  174 us (54%)
  local copies, waits for them, and re-layouts  85.5 us (27%)
  waiting for transfers between devices  23.2 us (7%)
  starting transfers between devices  19.8 us (6%)
  matrix products  9.93 us (3%)
    sub x1, other arithmetic, on_device(): return conserved - time_step * (y_term + z_final)  78.8 us
    concatenate x2, other arithmetic, extended(): jnp.concatenate([lax.ppermute(tail, axis, [(i, (i + 1) % count) for i in...  38.2 us
    add x2, other arithmetic, directed_flux(): return result + energy_pick * (pressure * velocity)[None]  28.8 us
    all_to_all x1, waiting for transfers between devices, on_device(): lax.all_to_all(outgoing, 'gx', split_axis=1, concat_axis=1, tiled=True)  16.2 us
    gather x2, local copies, waits for them, and re-layouts, on_device(): picked = jnp.take(replaced, slot_of, axis=1).reshape(z_term.shape)  15.2 us
    reshape x1, local copies, waits for them, and re-layouts, on_device(): wide_rows = widened.reshape(VARIABLES, cells_x * (cells_y + 6), cells_z + 6)  13.7 us
    gather x2, local copies, waits for them, and re-layouts, framed_pencils(): return jnp.take(wide_rows, rows, axis=1)  12.1 us
    sub x1, local copies, waits for them, and re-layouts, on_device(): return conserved - time_step * (y_term + z_final)  12 us
  transfers between devices with their start and end apart: 6, of which 2 were waited for; matrix products, arithmetic and copies ran while one was open for 21% of the time, Pallas kernels for 0%

commit v1 on v0

v1 whole, which is shorter than its diff:
```python
import functools

import jax
import jax.numpy as jnp
import numpy as np
from jax import lax
from jax.experimental import pallas as pl
from jax.experimental.pallas import tpu as pltpu
from jax.sharding import PartitionSpec as P

SPECIES = 9
VARIABLES = 14
CX, CY, CZ = 8, 64, 256
ROWS = CX * CY
PENCILS = 128
GROUP = 16
SIZE = VARIABLES * GROUP
CELLS = 280
TILES = 33
EPS = 0.75e-6
SCALE = 0.2 / 60.0

F32 = jnp.float32
BF16 = jnp.bfloat16
VMEM = pl.BlockSpec(memory_space=pltpu.VMEM)
SMEM = pl.BlockSpec(memory_space=pltpu.SMEM)
ANY = pl.BlockSpec(memory_space=pl.ANY)


def lanes(shape):
    return lax.broadcasted_iota(jnp.int32, shape, len(shape) - 1)


def split(values):
    high = values.astype(BF16)
    low = (values - high.astype(F32)).astype(BF16)
    return high, low


def dot(left, right):
    return jnp.dot(left, right, preferred_element_type=F32)


def state_of(read):
    density = read(0)
    for v in range(1, SPECIES):
        density = density + read(v)
    inverse = 1.0 / density
    m0, m1, m2 = read(9), read(10), read(11)
    squares = m0 * m0 + m1 * m1 + m2 * m2
    pressure = 0.4 * (read(12) - read(13) - 0.5 * squares * inverse)
    return m1 * inverse, m2 * inverse, pressure


def flux(value, velocity, pressure, v, normal):
    if v == SPECIES + 3:
        return (value + pressure) * velocity
    if v == SPECIES + normal:
        return value * velocity + pressure
    return value * velocity


def expand(matrix, scale, target):
    row = lax.broadcasted_iota(jnp.int32, (SIZE, SIZE), 0)
    column = lax.broadcasted_iota(jnp.int32, (SIZE, SIZE), 1)
    same = (row & (GROUP - 1)) == (column & (GROUP - 1))
    spread = (
        lax.broadcasted_iota(jnp.int32, (SIZE, VARIABLES), 0) // GROUP
        == lax.broadcasted_iota(jnp.int32, (SIZE, VARIABLES), 1)
    ).astype(BF16)
    gather = (
        lax.broadcasted_iota(jnp.int32, (VARIABLES, SIZE), 1) // GROUP
        == lax.broadcasted_iota(jnp.int32, (VARIABLES, SIZE), 0)
    ).astype(BF16)
    for part, places in zip(split(scale * matrix), ((0, 1), (2,))):
        wide = dot(spread, dot(part, gather).astype(BF16))
        wide = jnp.where(same, wide, 0.0).astype(BF16)
        for place in places:
            target[:, SIZE * place : SIZE * place + SIZE] = wide


def project(matrix, values):
    high, low = split(values)
    return dot(matrix[...], jnp.concatenate([high, low, high], axis=0))


def prepare_body(
    list_ref, where_ref, left_ref, right_ref, u_hbm,
    proj, velocity_ref, pressure_ref, speed_ref, yflux, zflux, kr_out,
    u_ref, rows_ref, cells, kl_ref, up_send, down_send, z_send, y_recv, z_recv,
    load_sems, send_sems, recv_sems,
):
    loads = []

    def load(index, t, x, y):
        copy = pltpu.make_async_copy(
            u_hbm.at[:, x, y, pl.ds(128 * t, 128)], u_ref.at[t, :, x, y], load_sems.at[index]
        )
        copy.start()
        loads.append(copy)

    every = pl.ds(0, CX)
    for t in range(2):
        load(len(loads), t, every, pl.ds(0, 8))
        load(len(loads), t, every, pl.ds(CY - 8, 8))
    for x in range(CX):
        for t in range(2):
            load(len(loads), t, pl.ds(x, 1), pl.ds(8, CY - 16))

    gy, gz = lax.axis_index("gy"), lax.axis_index("gz")
    ny = lax.axis_size("gy")
    above, below = {"gy": lax.rem(gy + 1, ny)}, {"gy": lax.rem(gy + ny - 1, ny)}
    beside = {"gz": 1 - gz}
    barrier = pltpu.get_barrier_semaphore()
    for device in (above, below, beside):
        pl.semaphore_signal(barrier, inc=1, device_id=device, device_id_type=pl.DeviceIdType.MESH)

    def remote(index, source, target, device):
        return pltpu.make_async_remote_copy(
            src_ref=source,
            dst_ref=target,
            send_sem=send_sems.at[index],
            recv_sem=recv_sems.at[index],
            device_id=device,
            device_id_type=pl.DeviceIdType.MESH,
        )

    for copy in loads[:4]:
        copy.wait()

    def y_ends(v, carry):
        for t in range(2):
            for x in range(CX):
                down_send[t, v, 3 * x : 3 * x + 3, :] = u_ref[t, v, x, 0:3, :]
                up_send[t, v, 3 * x : 3 * x + 3, :] = u_ref[t, v, x, CY - 3 : CY, :]
        return carry

    lax.fori_loop(0, VARIABLES, y_ends, 0)
    expand(left_ref[...], 0.5, kl_ref)
    expand(right_ref[...], 60.0, kr_out)
    pl.semaphore_wait(barrier, 3)
    up = remote(0, up_send, y_recv.at[0], above)
    down = remote(1, down_send, y_recv.at[1], below)
    up.start()
    down.start()

    lane = lanes((CY, 128))
    for x in range(CX):
        loads[4 + 2 * x].wait()
        loads[5 + 2 * x].wait()

        def z_ends(v, carry, x=x):
            ends = jnp.where(lane < 64, u_ref[0, v, x], u_ref[1, v, x])
            ends = pltpu.roll(ends, 16 * x + 3, 1)
            if x == 0:
                z_send[v] = ends
            else:
                z_send[v] = jnp.where(lane < 16 * x, z_send[v], ends)
            return carry

        lax.fori_loop(0, VARIABLES, z_ends, 0, unroll=2)

    flat = u_ref.reshape(2, VARIABLES * ROWS, 128)
    packed = rows_ref.reshape(2, VARIABLES * PENCILS, 128)

    def gather(p, carry):
        row = list_ref[p]
        for t in range(2):
            for v in range(VARIABLES):
                packed[t, pl.ds(p + v * PENCILS, 1), :] = flat[t, pl.ds(row + v * ROWS, 1), :]
        return carry

    lax.fori_loop(0, 8, gather, 0, unroll=2)
    ends = remote(2, z_send, z_recv, beside)
    ends.start()
    lax.fori_loop(8, PENCILS, gather, 0, unroll=2)

    def turn(v, carry):
        for t in range(2):
            cells[v, 8 + 128 * t : 136 + 128 * t, :] = rows_ref[t, v].T
        return carry

    lax.fori_loop(0, VARIABLES, turn, 0)

    def wave(i, peak):
        rows = pl.ds(pl.multiple_of(8 * i, 8), 8)
        _, velocity, pressure = state_of(lambda v: cells[v, rows, :])
        velocity_ref[rows, :] = velocity
        pressure_ref[rows, :] = pressure
        return jnp.maximum(peak, jnp.abs(velocity))

    peak = lax.fori_loop(1, 33, wave, jnp.zeros((8, 128), F32), unroll=2)

    def chunk(i, carry):
        first = pl.ds(pl.multiple_of(32 * i + 8, 8), 16)
        second = pl.ds(pl.multiple_of(32 * i + 24, 8), 16)
        values = jnp.concatenate([cells[:, first, :], cells[:, second, :]], axis=-1)
        result = project(kl_ref, values.reshape(SIZE, 256))
        proj[:, first, :] = result[:, 0:128].reshape(VARIABLES, 16, 128)
        proj[:, second, :] = result[:, 128:256].reshape(VARIABLES, 16, 128)
        return carry

    lax.fori_loop(0, CZ // 32, chunk, 0)

    ends.wait()
    halo_rows = z_recv.reshape(VARIABLES * CY, 128)
    fetched = rows_ref.at[0].reshape(VARIABLES * PENCILS, 128)

    def fetch(p, carry):
        y = list_ref[p] % CY
        for v in range(VARIABLES):
            fetched[pl.ds(p + v * PENCILS, 1), :] = halo_rows[pl.ds(y + v * CY, 1), :]
        return carry

    lax.fori_loop(0, PENCILS, fetch, 0, unroll=2)
    own_x = jnp.broadcast_to(where_ref[...] // CY, (16, 128))

    def turn_ends(v, carry):
        turned = rows_ref[0, v].T
        near = turned[0:16]
        for x in range(1, CX):
            near = jnp.where(own_x == x, turned[16 * x : 16 * x + 16], near)
        cells[v, 0:5, :] = near[0:5]
        cells[v, 5:8, :] = near[0:3]
        cells[v, 264:267, :] = near[3:6]
        cells[v, 267:272, :] = near[0:5]
        return carry

    lax.fori_loop(0, VARIABLES, turn_ends, 0, unroll=2)
    peak = wave(0, peak)
    peak = wave(33, peak)
    speed_ref[...] = jnp.broadcast_to(jnp.max(peak, axis=0, keepdims=True) + 1.0, (8, 128))
    values = jnp.concatenate([cells[:, 0:8, :], cells[:, 264:272, :]], axis=1)
    result = project(kl_ref, values.reshape(SIZE, 128)).reshape(VARIABLES, 16, 128)
    proj[:, 0:8, :] = result[:, 0:8]
    proj[:, 264:272, :] = result[:, 8:16]

    _, velocity, pressure = state_of(lambda v: z_recv[v])
    for v in range(VARIABLES):
        high, low = split(flux(z_recv[v], velocity, pressure, v, 2))
        zflux[v, :, 0:128] = high
        zflux[v, :, 128:256] = low

    up.wait()
    down.wait()
    for side in range(2):
        for t in range(2):
            velocity, _, pressure = state_of(lambda v: y_recv[side, t, v])
            for v in range(VARIABLES):
                yflux[side, t, v] = flux(y_recv[side, t, v], velocity, pressure, v, 1)


def prepare(shocked, left, right, conserved):
    return pl.pallas_call(
        prepare_body,
        out_shape=(
            jax.ShapeDtypeStruct((VARIABLES, CELLS, 128), F32),
            jax.ShapeDtypeStruct((CELLS, 128), F32),
            jax.ShapeDtypeStruct((CELLS, 128), F32),
            jax.ShapeDtypeStruct((8, 128), F32),
            jax.ShapeDtypeStruct((2, 2, VARIABLES, 3 * CX, 128), F32),
            jax.ShapeDtypeStruct((VARIABLES, CY, 256), BF16),
            jax.ShapeDtypeStruct((SIZE, 3 * SIZE), BF16),
        ),
        in_specs=[SMEM, VMEM, VMEM, VMEM, ANY],
        out_specs=(VMEM,) * 7,
        scratch_shapes=[
            pltpu.VMEM((2, VARIABLES, CX, CY, 128), F32),
            pltpu.VMEM((2, VARIABLES, PENCILS, 128), F32),
            pltpu.VMEM((VARIABLES, 272, 128), F32),
            pltpu.VMEM((SIZE, 3 * SIZE), BF16),
            pltpu.VMEM((2, VARIABLES, 3 * CX, 128), F32),
            pltpu.VMEM((2, VARIABLES, 3 * CX, 128), F32),
            pltpu.VMEM((VARIABLES, CY, 128), F32),
            pltpu.VMEM((2, 2, VARIABLES, 3 * CX, 128), F32),
            pltpu.VMEM((VARIABLES, CY, 128), F32),
            pltpu.SemaphoreType.DMA((4 + 2 * CX,)),
            pltpu.SemaphoreType.DMA((3,)),
            pltpu.SemaphoreType.DMA((3,)),
        ],
        compiler_params=pltpu.CompilerParams(collective_id=0, has_side_effects=True),
        name="prepare",
    )(shocked, shocked.reshape(1, PENCILS), left, right, conserved)


def weno_terms(columns_ref, proj, velocity_ref, pressure_ref, speed_ref, kr_ref, scratch):
    plus_ref, minus_ref, terms, sums, across, terms_out = scratch
    speed = speed_ref[...]

    def component(v, carry):
        pull, push = columns_ref[v, 0], columns_ref[v, 1]

        def fluxes(i, carry):
            rows = pl.ds(pl.multiple_of(8 * i, 8), 8)
            velocity = velocity_ref[rows, :]
            base = proj[v, rows, :]
            source = pressure_ref[rows, :] * (pull + velocity * push)
            plus_ref[rows, :] = (velocity + speed) * base + source
            minus_ref[rows, :] = (velocity - speed) * base + source
            return carry

        lax.fori_loop(0, 34, fluxes, 0, unroll=2)

        def pairs(i, carry):
            row = pl.multiple_of(8 * i, 8)
            for side, source in enumerate((plus_ref, minus_ref)):
                middle = source[pl.ds(row + 6, 8), :]
                x = middle - source[pl.ds(row + 5, 8), :]
                y = source[pl.ds(row + 7, 8), :] - middle
                xx, xy, yy = x * x, x * y, y * y
                ex, ey = xx + EPS, yy + EPS
                cross = 2.75 * xy
                lean = 1.0 / ((ex + 2.5 * yy) - cross)
                even = 1.0 / ((ex + yy) - 1.25 * xy)
                back = 1.0 / ((2.5 * xx + ey) - cross)
                x2, y2 = x + x, y + y
                if side == 0:
                    w0, w1, w2 = lean * lean, 6.0 * (even * even), 3.0 * (back * back)
                    n0, n1, n2 = 5.0 * y - x2, x + y2, (x2 + x2) - y
                else:
                    w0, w1, w2 = back * back, 6.0 * (even * even), 3.0 * (lean * lean)
                    n0, n1, n2 = 5.0 * x - y2, y + x2, (y2 + y2) - x
                for k, value in enumerate((w0, w1, w2, w0 * n0, w1 * n1, w2 * n2)):
                    terms[6 * side + k, pl.ds(row, 8), :] = value
            return carry

        lax.fori_loop(0, TILES, pairs, 0, unroll=3)

        def faces(i, carry):
            row = pl.multiple_of(8 * i, 8)

            def at(k, by):
                return terms[k, pl.ds(row + by, 8), :]

            gain = (at(3, 0) + at(4, 1) + at(5, 2)) / (at(0, 0) + at(1, 1) + at(2, 2))
            loss = (at(9, 3) + at(10, 2) + at(11, 1)) / (at(6, 3) + at(7, 2) + at(8, 1))
            base = plus_ref[pl.ds(row + 7, 8), :] + minus_ref[pl.ds(row + 8, 8), :]
            sums[v, pl.ds(row, 8), :] = base + (gain - loss) * (1.0 / 6.0)
            return carry

        lax.fori_loop(0, TILES, faces, 0, unroll=3)
        return carry

    lax.fori_loop(0, VARIABLES, component, 0)

    def chunk(i, carry):
        start = pl.multiple_of(32 * i, 8)

        def change(by):
            return sums[:, pl.ds(start + by + 1, 16), :] - sums[:, pl.ds(start + by, 16), :]

        values = jnp.concatenate([change(0), change(16)], axis=-1)
        result = project(kr_ref, values.reshape(SIZE, 256))
        for k in range(2):
            rows = pl.ds(pl.multiple_of(start + 16 * k, 8), 16)
            across[:, rows, :] = result[:, 128 * k : 128 * k + 128].reshape(VARIABLES, 16, 128)
        return carry

    lax.fori_loop(0, CZ // 32, chunk, 0)

    def turn_back(v, carry):
        for t in range(2):
            terms_out[t, v] = across[v, 128 * t : 128 * t + 128, :].T
        return carry

    lax.fori_loop(0, VARIABLES, turn_back, 0)


def advance_body(
    list_ref, count_ref, columns_ref, u_ref,
    proj, velocity_ref, pressure_ref, speed_ref, yflux, zflux, kr_ref, zcoef_ref, hcoef_ref,
    out_ref,
    hx_ref, replaced, mask_ref, v1_ref, p_ref, stage, along_z, along_y, *scratch,
):
    x = pl.program_id(0)

    @pl.when(x == 0)
    def _():
        weno_terms(columns_ref, proj, velocity_ref, pressure_ref, speed_ref, kr_ref, scratch)
        hx_ref[...] = jnp.zeros((256, CZ), BF16)
        mask_ref[...] = jnp.zeros((ROWS, 128), F32)
        flat = replaced.reshape(2, VARIABLES * ROWS, 128)
        packed = scratch[-1].reshape(2, VARIABLES * PENCILS, 128)

        def scatter(p, carry):
            row = list_ref[p]
            mask_ref[pl.ds(row, 1), :] = jnp.ones((1, 128), F32)
            for t in range(2):
                for v in range(VARIABLES):
                    flat[t, pl.ds(row + v * ROWS, 1), :] = packed[t, pl.ds(p + v * PENCILS, 1), :]
            return carry

        lax.fori_loop(0, count_ref[0], scatter, 0)

    @pl.when(x > 0)
    def _():
        for part in range(2):
            old = pl.ds(pl.multiple_of(128 * part + 16 * x - 16, 16), 16)
            hx_ref[old, :] = jnp.zeros((16, CZ), BF16)

    for part in range(2):
        new = pl.ds(pl.multiple_of(128 * part + 16 * x, 16), 16)
        hx_ref[new, :] = hcoef_ref[...]

    for t in range(2):
        cut = slice(128 * t, 128 * t + 128)
        velocity1, velocity2, pressure = state_of(lambda v: u_ref[v, 0, :, cut])
        v1_ref[t] = velocity1
        p_ref[t] = pressure
        for v in range(VARIABLES):
            high, low = split(flux(u_ref[v, 0, :, cut], velocity2, pressure, v, 2))
            stage[v, :, cut] = high
            stage[v, :, 256 + 128 * t : 384 + 128 * t] = low

    rows = VARIABLES * CY
    along_z[...] = dot(
        jnp.concatenate([stage[...].reshape(rows, 512), zflux[...].reshape(rows, 256)], axis=1),
        jnp.concatenate([zcoef_ref[...], zcoef_ref[...], hx_ref[...]], axis=0),
    ).reshape(VARIABLES, CY, CZ)

    hit = mask_ref[pl.ds(pl.multiple_of(CY * x, CY), CY), :] > 0.5
    for v in range(VARIABLES):
        for t in range(2):
            cut = slice(128 * t, 128 * t + 128)
            buffer = along_y.at[v % 2, t]
            value = u_ref[v, 0, :, cut]
            buffer[5:8, :] = yflux[0, t, v, pl.ds(3 * x, 3), :]
            buffer[8:72, :] = flux(value, v1_ref[t], p_ref[t], v, 1)
            buffer[72:75, :] = yflux[1, t, v, pl.ds(3 * x, 3), :]

            def at(by):
                return buffer[8 + by : 72 + by, :]

            y_term = 45.0 * (at(1) - at(-1)) - 9.0 * (at(2) - at(-2)) + (at(3) - at(-3))
            z_term = jnp.where(hit, replaced[t, v, x], along_z[v, :, cut])
            out_ref[v, 0, :, cut] = value - SCALE * (y_term + z_term)


def advance(shocked, live_count, columns, conserved, prepared, coefs):
    block = pl.BlockSpec((VARIABLES, 1, CY, CZ), lambda x: (0, x, 0, 0))
    return pl.pallas_call(
        advance_body,
        grid=(CX,),
        out_shape=jax.ShapeDtypeStruct(conserved.shape, F32),
        in_specs=[SMEM, SMEM, SMEM, block] + [VMEM] * 9,
        out_specs=block,
        scratch_shapes=[
            pltpu.VMEM((256, CZ), BF16),
            pltpu.VMEM((2, VARIABLES, CX, CY, 128), F32),
            pltpu.VMEM((ROWS, 128), F32),
            pltpu.VMEM((2, CY, 128), F32),
            pltpu.VMEM((2, CY, 128), F32),
            pltpu.VMEM((VARIABLES, CY, 512), BF16),
            pltpu.VMEM((VARIABLES, CY, CZ), F32),
            pltpu.VMEM((2, 2, 80, 128), F32),
            pltpu.VMEM((CELLS, 128), F32),
            pltpu.VMEM((CELLS, 128), F32),
            pltpu.VMEM((12, CELLS, 128), F32),
            pltpu.VMEM((VARIABLES, CELLS, 128), F32),
            pltpu.VMEM((VARIABLES, CZ, 128), F32),
            pltpu.VMEM((2, VARIABLES, PENCILS, 128), F32),
        ],
        name="advance",
    )(shocked, live_count, columns, conserved, *prepared, *coefs)


@functools.cache
def coefficients():
    weight = {1: 45.0, -1: -45.0, 2: -9.0, -2: 9.0, 3: 1.0, -3: -1.0}

    def coef(offset):
        return weight.get(offset, 0.0)

    zcoef = np.array([[coef(c - k) for k in range(CZ)] for c in range(CZ)])
    cells = [-3, -2, -1, CZ, CZ + 1, CZ + 2]
    hcoef = np.zeros((16, CZ))
    for j, c in enumerate(cells):
        for k in range(CZ):
            hcoef[j, k] = coef(c - k)
    return zcoef, hcoef


def on_device(conserved, char_left, char_right, shock_list, shock_count):
    shocked = shock_list.reshape(PENCILS)
    live_count = shock_count.reshape(1)
    prepared = prepare(shocked, char_left, char_right, conserved)
    columns = 0.5 * char_left[:, SPECIES + 2 : SPECIES + 4]
    coefs = [jnp.asarray(m, BF16) for m in coefficients()]
    return advance(shocked, live_count, columns, conserved, prepared, coefs)


def solution(mesh):
    placed = (P(None, "gx", "gy", "gz"), P(), P(), P("gx", "gy", "gz", None), P("gx", "gy", "gz"))
    return jax.shard_map(
        on_device, mesh=mesh, in_specs=placed, out_specs=P(None, "gx", "gy", "gz"), check_vma=False
    )
```

time: 320 us -> 52.4 us (0.16); the launches traced: 314 us -> 51.8 us
  other arithmetic: 174 us -> 1.36 us
  local copies, waits for them, and re-layouts: 85.5 us -> 0 us
  Pallas kernels: 0 us -> 49.8 us
  waiting for transfers between devices: 23.2 us -> 0 us
  starting transfers between devices: 19.8 us -> 0 us
  matrix products: 9.93 us -> 0 us
    sub x2 -> x0, other arithmetic: 79.1 us -> none  [the longest x1 78.8 us: on_device(): return conserved - time_step * (y_term + z_final)]
    pallas_call x0 -> x2, Pallas kernels: none -> 49.8 us  [the longest x1 29.7 us: advance(): pl.pallas_call(advance_body, grid=(CX,), out_shape=jax.ShapeDtypeStruct(c...]
    concatenate x3 -> x0, other arithmetic: 39.9 us -> none  [the longest x2 38.2 us: extended(): jnp.concatenate([lax.ppermute(tail, axis, [(i, (i + 1) % count) for i in...]
    add x3 -> x0, other arithmetic: 28.8 us -> none  [the longest x2 28.8 us: directed_flux(): return result + energy_pick * (pressure * velocity)[None]]
    gather x5 -> x0, local copies, waits for them, and re-layouts: 28.6 us -> none  [the longest x2 15.2 us: on_device(): picked = jnp.take(replaced, slot_of, axis=1).reshape(z_term.shape)]
    all_to_all x2 -> x0, waiting for transfers between devices: 23.2 us -> none  [the longest x1 16.2 us: on_device(): lax.all_to_all(outgoing, 'gx', split_axis=1, concat_axis=1, tiled=True)]
    reduce_sum x9 -> x0, other arithmetic: 17.1 us -> none  [the longest x3 11 us: directed_flux(): density = jnp.sum(values_in[:SPECIES], axis=0)]
    ppermute x2 -> x0, local copies, waits for them, and re-layouts: 15.3 us -> none  [the longest x1 7.65 us: extended(): lax.ppermute(head, axis, [((i + 1) % count, i) for i in range(count)])]
  transfers between devices with their start and end apart: 6 -> 0, of which waited for: 2 -> 0; matrix products, arithmetic and copies ran while one was open for 21% -> 0% of each run, Pallas kernels for 0% -> 0%
where the time goes in v1:
time: 52.4 us; the launch traced here: 51.8 us
  Pallas kernels  49.8 us (95%)
  other arithmetic  1.36 us (3%)
  between operations  0.66 us (1%)
    pallas_call x1, Pallas kernels, advance(): pl.pallas_call(advance_body, grid=(CX,), out_shape=jax.ShapeDtypeStruct(c...  29.7 us
    pallas_call x1, Pallas kernels, prepare(): pl.pallas_call(prepare_body, out_shape=(jax.ShapeDtypeStruct((VARIABLES,...  20 us
    mul x1, other arithmetic, on_device(): columns = 0.5 * char_left[:, SPECIES + 2:SPECIES + 4]  1.36 us

profile of v1, /device:TPU:3, one launch (start us, length us, event | category | flops | bytes accessed | tf_op | source)
XLA Modules:
  0.0 51.8 jit_solution(8438298801065496138)
XLA Ops:
  0.7 1.4 %slice_multiply_fusion.columns_ref = f32[14,2]{1,0:T(8,128)} fusion(f32[14,14]{1,0:T(8,128)} %left_ref.1), kind=kLoop, calls=%fused_computation | loop fusion | flops 28 | bytes 224 | tf_op jit(solution)/shard_map/mul | solution.py:487
  2.0 20.0 %prepare.1 = (f32[14,280,128]{2,1,0:T(8,128)}, f32[280,128]{1,0:T(8,128)}, f32[280,128]{1,0:T(8,128)}, f32[8,128]{1,0:T(8,128)}, f32[2,2,14,24,128]{4,3,2,1,0:T(...) custom-call(s32[128]{0:T(128)} %bitcast.4, s32[1,128]{1,0:T(1,128)} %bitcast.5, f32[14,14]{1,0:T(8,128)} %left_ref.1, ...), custom_call_target="tpu_custom_call" | custom-call | tf_op jit(solution)/shard_map/prepare/pallas_call | solution.py:254
  22.0 29.7 %advance.1 = f32[14,8,64,256]{3,2,1,0:T(8,128)} custom-call(s32[128]{0:T(128)} %bitcast.6, s32[1]{0:T(128)} %bitcast.3.count_ref, f32[14,2]{1,0:T(8,128)} %slice_multiply_fusion.columns_ref, f32[14,8,64,256]{3,2,1,0:T(8,128)} %u_ref.1, f32[14,280,128]{2,1,0:T(8,128)} %get-tuple-element.12.proj, f32[280,128]{1,0:T(8,128)} %get-tuple-element.13.velocity_ref, ...), custom_call_target="tpu_custom_call" | custom-call | tf_op jit(solution)/shard_map/advance/pallas_call | solution.py:441
